TPU v7x, 32 devices: a whole 2x2x4 slice. The times are simulated.
32 devices in a mesh: ens: 2 (over y), bfly: 4 (over z), cblk: 4 (over x, core).
Axes of the slice: x: 2, y: 2, z: 4, core: 2. Of those that a mesh axis runs over, the one named last changes fastest.
Arguments:
- source: bfloat16 [65536, 512], P(('ens', 'bfly', 'cblk')), parts along dimension 0, may hold values from -6 to 6
- basis: bfloat16 [65536, 256], P(('ens', 'bfly', 'cblk')), parts along dimension 0, may hold values from -0.0625 to 0.0625
- transfer: bfloat16 [4, 4, 256, 512], P('ens', 'bfly'), parts along dimension 0, may hold values from -0.25 to 0.25
- skeleton: int32 [32, 16], P(('ens', 'bfly', 'cblk')), parts along dimension 0, may hold values from 0 to 15, each once within a row
- row_class: int32 [65536], P(('ens', 'bfly', 'cblk')), parts along dimension 0, may hold values from 0 to 15
- linear_table: float32 [16, 512], replicated, may hold values from 0.5 to 1.5
- cubic_table: float32 [16, 512], replicated, may hold values from 0.05 to 0.3
Outputs:
- adjoint: bfloat16 [65536, 512], P(('ens', 'bfly', 'cblk')), parts along dimension 0
There are 2 independent parts, one for each index of `ens`. A program takes and returns all parts, laid end to end along the dimension named above; an argument that names none is the same for every part. Nothing has to cross between parts.
Inputs may be any that keep to these rules, and one draw needn't show every extreme that they name: Each row of skeleton names each of the 16 tiles once.
All inputs are finite; a program needn't handle non-finite values.
Results may differ from a plain program's by a relative error of at most 0.0052.
Values may be sent and summed in bfloat16 or wider, within the bound.
A program may use at most 64 MiB of HBM per device.

v0:
```python
import math

import jax
import jax.numpy as jnp
from jax import lax
from jax.sharding import PartitionSpec as P


def from_partner(array, axis, bit):
    return lax.ppermute(array, axis, [(i, i ^ 1 << bit) for i in range(lax.axis_size(axis))])


def times_transposed(left, right):
    dims = (((1,), (1,)), ((), ()))
    return lax.dot_general(
        left,
        right.astype(jnp.float32),
        dims,
        precision=lax.Precision.HIGHEST,
        preferred_element_type=jnp.float32,
    )


def times_plain(left, right):
    return jnp.dot(
        left,
        right.astype(jnp.float32),
        precision=lax.Precision.HIGHEST,
        preferred_element_type=jnp.float32,
    )


def leaf_terms(data, basis):
    return lax.dot_general(
        data, basis, (((0,), (0,)), ((), ())), preferred_element_type=jnp.float32
    )


def expand_rows(basis, carried, factor_rho):
    return factor_rho * lax.dot_general(
        basis, carried, (((1,), (1,)), ((), ())), preferred_element_type=jnp.float32
    )


def forward_levels(coefficient, factors):
    rank_size = factors.shape[1]
    for level in range(factors.shape[0]):
        partner = from_partner(coefficient, "bfly", level)
        coefficient = times_transposed(
            coefficient, factors[level, :, :rank_size]
        ) + times_transposed(partner, factors[level, :, rank_size:])
    return coefficient


def adjoint_levels(coefficient, factors):
    rank_size = factors.shape[1]
    for level in reversed(range(factors.shape[0])):
        sending = times_plain(coefficient, factors[level, :, rank_size:])
        received = from_partner(sending, "bfly", level)
        coefficient = times_plain(coefficient, factors[level, :, :rank_size]) + received
    return coefficient


def per_device(source, basis, transfer, skeleton, row_class, linear_table, cubic_table):
    rows, columns = source.shape
    order = skeleton[0]
    tiles = order.shape[0]
    picked = jnp.take(source.reshape(tiles, rows // tiles, columns), order, axis=0).reshape(
        rows, columns
    )
    factors = transfer[:, 0]
    factor_rho = math.sqrt(rows * lax.axis_size("cblk") / basis.shape[1])
    summed = lax.psum(leaf_terms(picked, basis), "cblk")
    carried = forward_levels(summed, factors).astype(jnp.bfloat16)
    mapped = expand_rows(basis, carried, factor_rho)
    classes = jnp.arange(linear_table.shape[0], dtype=jnp.int32)
    one_hot = (row_class[:, None] == classes[None, :]).astype(jnp.float32)
    tables = jnp.concatenate([linear_table, cubic_table], axis=1)
    looked = jnp.dot(
        one_hot, tables, precision=lax.Precision.HIGHEST, preferred_element_type=jnp.float32
    )
    linear = looked[:, :columns]
    cubic = looked[:, columns:]
    weighted = (mapped * (linear + cubic * mapped * mapped)).astype(jnp.bfloat16)
    gathered = lax.psum_scatter(
        leaf_terms(weighted, basis), "cblk", scatter_dimension=0, tiled=True
    )
    returned = adjoint_levels(gathered, factors).astype(jnp.bfloat16)
    ordered = expand_rows(
        basis, lax.all_gather(returned, "cblk", axis=0, tiled=True), factor_rho
    ).astype(jnp.bfloat16)
    inverse = jnp.argsort(order)
    adjoint = jnp.take(ordered.reshape(tiles, rows // tiles, columns), inverse, axis=0)
    return adjoint.reshape(rows, columns)


def solution(mesh):
    placed = (
        P(("ens", "bfly", "cblk"), None),
        P(("ens", "bfly", "cblk"), None),
        P("ens", "bfly", None, None),
        P(("ens", "bfly", "cblk"), None),
        P(("ens", "bfly", "cblk")),
        P(),
        P(),
    )
    return jax.shard_map(
        per_device,
        mesh=mesh,
        in_specs=placed,
        out_specs=P(("ens", "bfly", "cblk"), None),
        check_vma=False,
    )
```

profile of v0, /device:TPU:0, one launch (start us, length us, event | category | flops | bytes accessed | tf_op | source)
XLA Modules:
  0.0 161.0 jit_solution(5023362638935786127)
XLA Ops:
  8.1 2.0 %gather_fusion = bf16[16,128,512]{2,1,0:T(8,128)(2,1)} fusion(bf16[16,128,512]{2,1,0:T(8,128)(2,1)S(1)} %bitcast.46, s32[1024]{0:T(1024)S(1)} %pad_clamp_fusion.1), kind=kCustom, calls=%fused_computation.clone | custom fusion | bytes 4194368 | tf_op jit(solution)/shard_map/jit(_take)/gather | solution.py:68
  10.1 1.9 %broadcast_select_fusion.1 = bf16[16,128,512]{2,1,0:T(8,128)(2,1)S(1)} fusion(bf16[16,128,512]{2,1,0:T(8,128)(2,1)} %gather_fusion, pred[16]{0:T(512)(128)(4,1)S(1)} %compare_and_fusion.1), kind=kLoop, calls=%fused_computation.9 | loop fusion | flops 1048576 | bytes 4194320 | tf_op jit(solution)/shard_map/jit(_take)/select_n | solution.py:68
  12.1 1.5 fusion.18
  13.7 36.2 %all-reduce.2.cloned.1.call-done = f32[512,256]{1,0:T(8,128)} async-done(((f32[512,256]{1,0:T(8,128)}), f32[512,256]{1,0:T(8,128)}) %all-reduce.2.cloned.1.call-update) | async-done | bytes 524304 | tf_op jit(solution)/shard_map/psum | solution.py:73
  50.0 1.5 collective-permute-start
  51.5 1.5 fusion.9
  52.9 9.7 %collective-permute-done = f32[512,256]{1,0:T(8,128)S(1)} collective-permute-done((f32[512,256]{1,0:T(8,128)}, f32[512,256]{1,0:T(8,128)S(1)}, u32[]{:S(2)}, u32[]{:S(2)}) %collective-permute-start) | collective-permute-done | bytes 524320 | tf_op jit(solution)/shard_map/ppermute | solution.py:10
  62.7 1.3 convolution_add_fusion.1
  64.0 2.7 %collective-permute-start.1 = (f32[512,256]{1,0:T(8,128)S(1)}, f32[512,256]{1,0:T(8,128)S(1)}, u32[]{:S(2)}, u32[]{:S(2)}) collective-permute-start(f32[512,256]{1,0:T(8,128)S(1)} %convolution_add_fusion.1), channel_id=1, source_target_pairs={{0,8},{4,12},{8,0},{12,4},{1,9},{5,13},{9,1},{13,5},{2,10},{6,14},... | collective-permute-start | bytes 1572872 | tf_op jit(solution)/shard_map/ppermute | solution.py:10
  66.7 5.8 %fusion.7 = f32[2048,1024]{0,1:T(8,128)} fusion(s32[2048]{0:T(1024)S(1)} %copy-done.3, f32[16,512]{1,0:T(8,128)S(1)} %copy-done.4, f32[16,512]{1,0:T(8,128)S(1)} %copy-done.5), kind=kOutput, calls=%fused_computation.18 | convolution fusion | flops 402702336 | bytes 8462336 | tf_op jit(solution)/shard_map/dot_general | solution.py:79
  73.0 15.1 %collective-permute-done.1 = f32[512,256]{1,0:T(8,128)S(1)} collective-permute-done((f32[512,256]{1,0:T(8,128)S(1)}, f32[512,256]{1,0:T(8,128)S(1)}, u32[]{:S(2)}, u32[]{:S(2)}) %collective-permute-start.1) | collective-permute-done | bytes 524320 | tf_op jit(solution)/shard_map/ppermute | solution.py:10
  88.5 5.7 %fusion.4 = f32[512,256]{1,0:T(8,128)} fusion(bf16[2048,256]{1,0:T(8,128)(2,1)S(1)} %copy-done.1, f32[2048,1024]{0,1:T(8,128)} %fusion.7, bf16[512,256]{1,0:T(8,128)(2,1)S(1)} %fusion.5), kind=kOutput, calls=%fused_computation.10 | convolution fusion | flops 1080033280 | bytes 11272192 | tf_op jit(solution)/shard_map/dot_general | solution.py:34
  94.2 1.3 sort.17
  95.5 21.5 %reduce-scatter.2.cloned.1.call-done = f32[128,256]{1,0:T(8,128)} async-done(((f32[512,256]{1,0:T(8,128)}), f32[128,256]{1,0:T(8,128)}) %reduce-scatter.2.cloned.1.call-update) | async-done | bytes 131088 | tf_op jit(solution)/shard_map/reduce_scatter | solution.py:85
  117.1 1.2 fusion.12
  118.3 2.5 %collective-permute-start.2 = (f32[128,256]{1,0:T(8,128)S(1)}, f32[128,256]{1,0:T(8,128)S(1)}, u32[]{:S(2)}, u32[]{:S(2)}) collective-permute-start(f32[128,256]{1,0:T(8,128)S(1)} %fusion.12), channel_id=1, source_target_pairs={{0,8},{4,12},{8,0},{12,4},{1,9},{5,13},{9,1},{13,5},{2,10},{6,14},... | collective-permute-start | bytes 393224 | tf_op jit(solution)/shard_map/ppermute | solution.py:10
  120.8 6.4 %collective-permute-done.2 = f32[128,256]{1,0:T(8,128)S(1)} collective-permute-done((f32[128,256]{1,0:T(8,128)S(1)}, f32[128,256]{1,0:T(8,128)S(1)}, u32[]{:S(2)}, u32[]{:S(2)}) %collective-permute-start.2) | collective-permute-done | bytes 131104 | tf_op jit(solution)/shard_map/ppermute | solution.py:10
  127.1 1.2 convolution_add_fusion.3
  130.0 4.5 %collective-permute-done.3 = f32[128,256]{1,0:T(8,128)S(1)} collective-permute-done((f32[128,256]{1,0:T(8,128)S(1)}, f32[128,256]{1,0:T(8,128)S(1)}, u32[]{:S(2)}, u32[]{:S(2)}) %collective-permute-start.3) | collective-permute-done | bytes 131104 | tf_op jit(solution)/shard_map/ppermute | solution.py:10
  135.6 5.8 %all_gather.3 = bf16[512,256]{1,0:T(8,128)(2,1)S(1)} all-gather(bf16[128,256]{1,0:T(8,128)(2,1)S(1)} %fusion.6), channel_id=1, replica_groups=mesh['ens'=2,'bfly'=4,'cblk'=4] {'cblk'}, dimensions={0}, use_global_device_ids=true | all-gather | bytes 327680 | tf_op jit(solution)/shard_map/all_gather | solution.py:90
  141.4 2.1 %fusion.3 = bf16[2048,512]{0,1:T(8,128)(2,1)} fusion(bf16[512,256]{1,0:T(8,128)(2,1)S(1)} %all_gather.3, bf16[2048,256]{1,0:T(8,128)(2,1)S(1)} %copy-done.1), kind=kOutput, calls=%fused_computation.7 | convolution fusion | flops 538968064 | bytes 3407872 | tf_op jit(solution)/shard_map/dot_general | solution.py:40
  143.5 3.9 %copy.15 = bf16[2048,512]{1,0:T(8,128)(2,1)} copy(bf16[2048,512]{0,1:T(8,128)(2,1)} %fusion.3) | data formatting | bytes 4194304 | tf_op jit(solution)/shard_map/reshape | solution.py:93
  147.4 3.6 %gather_fusion.1 = bf16[16,128,512]{2,1,0:T(8,128)(2,1)} fusion(bf16[16,128,512]{2,1,0:T(8,128)(2,1)} %bitcast.48, s32[1024]{0:T(1024)S(1)} %pad_clamp_fusion), kind=kCustom, calls=%fused_computation.1.clone | custom fusion | bytes 4194368 | tf_op jit(solution)/shard_map/jit(_take)/gather | solution.py:93
  151.0 3.2 %broadcast_select_fusion = bf16[16,128,512]{2,1,0:T(8,128)(2,1)} fusion(bf16[16,128,512]{2,1,0:T(8,128)(2,1)} %gather_fusion.1, pred[16]{0:T(512)(128)(4,1)S(1)} %compare_and_fusion), kind=kLoop, calls=%fused_computation.8 | loop fusion | flops 1048576 | bytes 4194320 | tf_op jit(solution)/shard_map/jit(_take)/select_n | solution.py:93
  (30 shorter events, 5.4 us)
Async XLA Ops:
  6.5 1.6 copy-start
  6.5 43.4 %all-reduce.2.cloned.1.call-start = ((), (), s32[]{:S(2)}) async-start(), calls=%async_computation.1 | async-start | bytes 1048576 | tf_op jit(solution)/shard_map/psum | solution.py:73
  10.1 2.0 %copy-start.1 = (bf16[2048,256]{1,0:T(8,128)(2,1)S(1)}, bf16[2048,256]{1,0:T(8,128)(2,1)}, u32[]{:S(2)}) copy-start(bf16[2048,256]{1,0:T(8,128)(2,1)} %param.10) | copy-start | bytes 3145732
  13.6 53.1 %copy-start.3 = (s32[2048]{0:T(1024)S(1)}, s32[2048]{0:T(1024)}, u32[]{:S(2)}) copy-start(s32[2048]{0:T(1024)} %param.13) | copy-start | bytes 24580
  13.6 53.1 %copy-start.4 = (f32[16,512]{1,0:T(8,128)S(1)}, f32[16,512]{1,0:T(8,128)}, u32[]{:S(2)}) copy-start(f32[16,512]{1,0:T(8,128)} %param.15) | copy-start | bytes 98308
  13.6 53.1 %copy-start.5 = (f32[16,512]{1,0:T(8,128)S(1)}, f32[16,512]{1,0:T(8,128)}, u32[]{:S(2)}) copy-start(f32[16,512]{1,0:T(8,128)} %param.14) | copy-start | bytes 98308
  13.7 103.4 %reduce-scatter.2.cloned.1.call-start = ((), (), s32[]{:S(2)}) async-start(), calls=%async_computation.2 | async-start | bytes 655360 | tf_op jit(solution)/shard_map/reduce_scatter | solution.py:85
  50.0 12.7 %collective-permute-start = (f32[512,256]{1,0:T(8,128)}, f32[512,256]{1,0:T(8,128)S(1)}, u32[]{:S(2)}, u32[]{:S(2)}) collective-permute-start(f32[512,256]{1,0:T(8,128)} %all-reduce.2.cloned.1.call-done), channel_id=1, source_target_pairs={{0,4},{4,0},{8,12},{12,8},{1,5},{5,1},{9,13},{13,9},{2,6},{6,2},{1... | collective-permute-start | bytes 1572872 | tf_op jit(solution)/shard_map/ppermute | solution.py:10
  64.0 8.6 %copy-start.2 = (bf16[2,1,256,512]{3,2,1,0:T(8,128)(2,1)S(1)}, bf16[2,1,256,512]{3,2,1,0:T(8,128)(2,1)}, u32[]{:S(2)}) copy-start(bf16[2,1,256,512]{3,2,1,0:T(8,128)(2,1)} %param.11) | copy-start | bytes 1572868
  64.0 24.1 %collective-permute-start.1 = (f32[512,256]{1,0:T(8,128)S(1)}, f32[512,256]{1,0:T(8,128)S(1)}, u32[]{:S(2)}, u32[]{:S(2)}) collective-permute-start(f32[512,256]{1,0:T(8,128)S(1)} %convolution_add_fusion.1), channel_id=1, source_target_pairs={{0,8},{4,12},{8,0},{12,4},{1,9},{5,13},{9,1},{13,5},{2,10},{6,14},... | collective-permute-start | bytes 1572872 | tf_op jit(solution)/shard_map/ppermute | solution.py:10
  88.5 5.7 %copy-start.6 = (s32[1,16]{1,0:T(1,128)S(1)}, s32[1,16]{1,0:T(1,128)}, u32[]{:S(2)}) copy-start(s32[1,16]{1,0:T(1,128)} %param.12) | copy-start | bytes 196
  118.3 8.9 %collective-permute-start.2 = (f32[128,256]{1,0:T(8,128)S(1)}, f32[128,256]{1,0:T(8,128)S(1)}, u32[]{:S(2)}, u32[]{:S(2)}) collective-permute-start(f32[128,256]{1,0:T(8,128)S(1)} %fusion.12), channel_id=1, source_target_pairs={{0,8},{4,12},{8,0},{12,4},{1,9},{5,13},{9,1},{13,5},{2,10},{6,14},... | collective-permute-start | bytes 393224 | tf_op jit(solution)/shard_map/ppermute | solution.py:10
  129.5 5.0 %collective-permute-start.3 = (f32[128,256]{1,0:T(8,128)S(1)}, f32[128,256]{1,0:T(8,128)S(1)}, u32[]{:S(2)}, u32[]{:S(2)}) collective-permute-start(f32[128,256]{1,0:T(8,128)S(1)} %fusion.10), channel_id=1, source_target_pairs={{0,4},{4,0},{8,12},{12,8},{1,5},{5,1},{9,13},{13,9},{2,6},{6,2},{1... | collective-permute-start | bytes 393224 | tf_op jit(solution)/shard_map/ppermute | solution.py:10
Sparse Core Ops, SparseCore 0:
  13.8 36.1 all-reduce.1
  94.3 22.7 reduce-scatter.1
where the time goes:
time: 161 us
  waiting for transfers between devices  93.4 us (58%)
  matrix products  23.4 us (15%)
  between operations  13.5 us (8%)
  local copies, waits for them, and re-layouts  9.65 us (6%)
  other arithmetic  7.91 us (5%)
  starting transfers between devices  7.28 us (5%)
  blocking collectives  5.78 us (4%)
    psum x1, waiting for transfers between devices, per_device(): summed = lax.psum(leaf_terms(picked, basis), 'cblk')  36.2 us
    ppermute x4, waiting for transfers between devices, from_partner(): lax.ppermute(array, axis, [(i, i ^ 1 << bit) for i in range(lax.axis_size...  35.6 us
    reduce_scatter x1, waiting for transfers between devices, per_device(): lax.psum_scatter(leaf_terms(weighted, basis), 'cblk', scatter_dimension=0...  21.5 us
    ppermute x4, starting transfers between devices, from_partner(): lax.ppermute(array, axis, [(i, i ^ 1 << bit) for i in range(lax.axis_size...  7.24 us
    dot_general x2, matrix products, leaf_terms(): lax.dot_general(data, basis, (((0,), (0,)), ((), ())), preferred_element_...  7.2 us
    dot_general x1, matrix products, per_device(): jnp.dot(one_hot, tables, precision=lax.Precision.HIGHEST, preferred_eleme...  5.84 us
    all_gather x1, blocking collectives, per_device(): lax.all_gather(returned, 'cblk', axis=0, tiled=True)  5.78 us
    dot_general x4, matrix products, times_plain(): jnp.dot(left, right.astype(jnp.float32), precision=lax.Precision.HIGHEST,...  4.67 us
  transfers between devices with their start and end apart: 6, of which 6 were waited for; matrix products, arithmetic and copies ran while one was open for 6% of the time, Pallas kernels for 0%

commit v1 on v0

v1 whole, which is shorter than its diff:
```python
import functools
import math

import jax
import jax.numpy as jnp
from jax import lax
from jax.experimental import pallas as pl
from jax.experimental.pallas import tpu as pltpu
from jax.sharding import PartitionSpec as P

MESH = pl.DeviceIdType.MESH
BF16, F32 = jnp.bfloat16, jnp.float32


def mm(left, right):
    return jnp.dot(left, right, preferred_element_type=F32)


def halves(value):
    high = value.astype(BF16)
    return high, (value - high.astype(F32)).astype(BF16)


def inverse_order(skeleton, tiles):
    order = [skeleton[0, i] for i in range(tiles)]
    inverse = []
    for j in range(tiles):
        place = jnp.int32(0)
        for i in range(1, tiles):
            place = jnp.where(order[i] == j, jnp.int32(i), place)
        inverse.append(place)
    return inverse


def core_kernel(
    n, levels, tiles, tile, rank, columns, rho,
    skeleton, classes, linear, cubic, source_any, basis_any, transfer_any,
    returned,
    source, basis, transfer, flipped, straight, turned, factors_t,
    lin, cub, weighted, whole,
    own32, part_out, part_in, level_out, level_in, share_out, share_in,
    local_sem, send_rs, recv_rs, send_lv, recv_lv, send_ag, recv_ag,
):
    share = columns // n
    rows = tiles * tile
    chunks = 4
    span = rows // chunks
    me = lax.axis_index("cblk")
    seat = lax.axis_index("bfly")

    def peer(k):
        return lax.rem(me + k, n)

    def partner(level):
        step = 1 << level
        return seat + (1 - 2 * lax.rem(seat // step, 2)) * step

    basis_copy = pltpu.make_async_copy(basis_any, basis, local_sem.at[0])
    basis_copy.start()
    source_copies = [
        pltpu.make_async_copy(
            source_any.at[pl.ds(c * span, span)], source.at[pl.ds(c * span, span)], local_sem.at[2 + c]
        )
        for c in range(chunks)
    ]
    for copy in source_copies:
        copy.start()
    transfer_copy = pltpu.make_async_copy(transfer_any, transfer, local_sem.at[1])
    transfer_copy.start()

    barrier = pltpu.get_barrier_semaphore()
    for k in range(1, n):
        pl.semaphore_signal(barrier, inc=1, device_id={"cblk": peer(k)}, device_id_type=MESH)
    for level in range(levels):
        pl.semaphore_signal(barrier, inc=1, device_id={"bfly": partner(level)}, device_id_type=MESH)

    inverse = inverse_order(skeleton, tiles)
    basis_copy.wait()
    for i in range(tiles):
        flipped[i] = basis[i].T
    for j in range(tiles):
        turned[:, j * tile:(j + 1) * tile] = flipped[inverse[j]]

    total = None
    for c in range(chunks):
        source_copies[c].wait()
        term = mm(turned[:, c * span:(c + 1) * span], source[c * span:(c + 1) * span, :])
        total = term if total is None else total + term

    def scatter(total, phase):
        for d in range(n):
            piece = total[:, d * share:(d + 1) * share]
            own32[d] = piece
            part_out[phase, d] = piece.astype(BF16)
        copies = []
        for k in range(1, n):
            copy = pltpu.make_async_remote_copy(
                src_ref=part_out.at[phase, peer(k)],
                dst_ref=part_in.at[phase, k - 1],
                send_sem=send_rs.at[phase, k - 1],
                recv_sem=recv_rs.at[phase, k - 1],
                device_id={"cblk": peer(k)},
                device_id_type=MESH,
            )
            copy.start()
            copies.append(copy)
        return copies

    def collect(copies, phase):
        value = own32[me]
        for k in range(1, n):
            copies[k - 1].wait()
            value = value + part_in[phase, k - 1].astype(F32)
        return value

    def exchange(phase, level):
        copy = pltpu.make_async_remote_copy(
            src_ref=level_out.at[phase, level],
            dst_ref=level_in.at[phase, level],
            send_sem=send_lv.at[phase, level],
            recv_sem=recv_lv.at[phase, level],
            device_id={"bfly": partner(level)},
            device_id_type=MESH,
        )
        copy.start()
        return copy

    def gather(value, phase):
        share_out[phase] = value.astype(BF16)
        share_in[phase, me] = value.astype(BF16)
        copies = []
        for k in range(1, n):
            copy = pltpu.make_async_remote_copy(
                src_ref=share_out.at[phase],
                dst_ref=share_in.at[phase, me],
                send_sem=send_ag.at[phase, k - 1],
                recv_sem=recv_ag.at[phase, k - 1],
                device_id={"cblk": peer(k)},
                device_id_type=MESH,
            )
            copy.start()
            copies.append(copy)
        return copies

    def assemble(copies, phase, target):
        for copy in copies:
            copy.wait()
        for d in range(n):
            target[:, d * share:(d + 1) * share] = share_in[phase, d]

    pl.semaphore_wait(barrier, n - 1 + levels)
    copies = scatter(total, 0)

    kinds = linear.shape[0]
    pieces = []
    for table in (linear[...], cubic[...]):
        high = table.astype(BF16)
        rest = table - high.astype(F32)
        middle = rest.astype(BF16)
        low = (rest - middle.astype(F32)).astype(BF16)
        pieces.append(jnp.concatenate([high, middle, low], axis=0))
    ids = lax.broadcasted_iota(jnp.int32, (kinds, tile), 0)
    for i in range(tiles):
        hot = jnp.where(classes[i:i + 1, :] == ids, F32(1), F32(0))
        hot = jnp.concatenate([hot, hot, hot], axis=0).T.astype(BF16)
        lin[i * tile:(i + 1) * tile, :] = mm(hot, pieces[0])
        cub[i * tile:(i + 1) * tile, :] = mm(hot, pieces[1])
        straight[:, i * tile:(i + 1) * tile] = flipped[i]
    transfer_copy.wait()
    for level in range(levels):
        factors_t[level] = transfer[level, 0].T

    value = collect(copies, 0)
    for level in range(levels):
        high, low = halves(value)
        level_out[0, level] = high
        copy = exchange(0, level)
        own = transfer[level, 0, :, :rank]
        value = mm(own, high) + mm(own, low)
        copy.wait()
        value = value + mm(transfer[level, 0, :, rank:], level_in[0, level])

    copies = gather(value, 0)
    assemble(copies, 0, whole)
    for c in range(chunks):
        at = slice(c * span, (c + 1) * span)
        left = basis[c * (tiles // chunks):(c + 1) * (tiles // chunks)].reshape(span, rank)
        mapped = rho * mm(left, whole[...])
        weighted[at, :] = (mapped * (lin[at, :] + cub[at, :] * mapped * mapped)).astype(BF16)
    back = mm(straight[...], weighted[...])

    copies = scatter(back, 1)
    value = collect(copies, 1)
    for level in reversed(range(levels)):
        high, low = halves(value)
        theirs = factors_t[level, rank:, :]
        level_out[1, level] = (mm(theirs, high) + mm(theirs, low)).astype(BF16)
        copy = exchange(1, level)
        own = factors_t[level, :rank, :]
        value = mm(own, high) + mm(own, low)
        copy.wait()
        value = value + level_in[1, level].astype(F32)
    copies = gather(value, 1)
    assemble(copies, 1, returned)


def expand_kernel(tiles, tile, rho, skeleton, basis, returned, out_any, ordered, sems):
    group = 2
    copies = []
    for g in range(tiles // group):
        left = basis[g * group * tile:(g + 1) * group * tile, :]
        value = (rho * mm(left, returned[...])).astype(BF16)
        for i in range(group):
            at = g * group + i
            ordered[at] = value[i * tile:(i + 1) * tile]
            copy = pltpu.make_async_copy(ordered.at[at], out_any.at[skeleton[0, at]], sems.at[at])
            copy.start()
            copies.append(copy)
    for copy in copies:
        copy.wait()


def per_device(source, basis, transfer, skeleton, row_class, linear_table, cubic_table):
    rows, columns = source.shape
    rank = basis.shape[1]
    tiles = skeleton.shape[1]
    tile = rows // tiles
    levels = transfer.shape[0]
    n = lax.axis_size("cblk")
    share = columns // n
    rho = math.sqrt(rows * n / rank)
    vmem = pl.BlockSpec(memory_space=pltpu.VMEM)
    smem = pl.BlockSpec(memory_space=pltpu.SMEM)
    anywhere = pl.BlockSpec(memory_space=pl.ANY)
    dma = pltpu.SemaphoreType.DMA
    returned = pl.pallas_call(
        functools.partial(core_kernel, n, levels, tiles, tile, rank, columns, rho),
        out_shape=jax.ShapeDtypeStruct((rank, columns), BF16),
        in_specs=[smem, vmem, vmem, vmem, anywhere, anywhere, anywhere],
        out_specs=vmem,
        scratch_shapes=[
            pltpu.VMEM((rows, columns), BF16),
            pltpu.VMEM((tiles, tile, rank), BF16),
            pltpu.VMEM(transfer.shape, BF16),
            pltpu.VMEM((tiles, rank, tile), BF16),
            pltpu.VMEM((rank, rows), BF16),
            pltpu.VMEM((rank, rows), BF16),
            pltpu.VMEM((levels, 2 * rank, rank), BF16),
            pltpu.VMEM((rows, columns), F32),
            pltpu.VMEM((rows, columns), F32),
            pltpu.VMEM((rows, columns), BF16),
            pltpu.VMEM((rank, columns), BF16),
            pltpu.VMEM((n, rank, share), F32),
            pltpu.VMEM((2, n, rank, share), BF16),
            pltpu.VMEM((2, n - 1, rank, share), BF16),
            pltpu.VMEM((2, levels, rank, share), BF16),
            pltpu.VMEM((2, levels, rank, share), BF16),
            pltpu.VMEM((2, rank, share), BF16),
            pltpu.VMEM((2, n, rank, share), BF16),
            dma((6,)),
            dma((2, n - 1)),
            dma((2, n - 1)),
            dma((2, levels)),
            dma((2, levels)),
            dma((2, n - 1)),
            dma((2, n - 1)),
        ],
        compiler_params=pltpu.CompilerParams(
            collective_id=0, has_side_effects=True, vmem_limit_bytes=48 << 20
        ),
        name="butterfly",
    )(
        skeleton,
        row_class.reshape(tiles, tile),
        linear_table,
        cubic_table,
        source,
        basis.reshape(tiles, tile, rank),
        transfer,
    )
    adjoint = pl.pallas_call(
        functools.partial(expand_kernel, tiles, tile, rho),
        out_shape=jax.ShapeDtypeStruct((tiles, tile, columns), BF16),
        in_specs=[smem, vmem, vmem],
        out_specs=anywhere,
        scratch_shapes=[pltpu.VMEM((tiles, tile, columns), BF16), dma((tiles,))],
        compiler_params=pltpu.CompilerParams(vmem_limit_bytes=24 << 20),
        name="expand",
    )(skeleton, basis, returned)
    return adjoint.reshape(rows, columns)


def solution(mesh):
    placed = (
        P(("ens", "bfly", "cblk"), None),
        P(("ens", "bfly", "cblk"), None),
        P("ens", "bfly", None, None),
        P(("ens", "bfly", "cblk"), None),
        P(("ens", "bfly", "cblk")),
        P(),
        P(),
    )
    return jax.shard_map(
        per_device,
        mesh=mesh,
        in_specs=placed,
        out_specs=P(("ens", "bfly", "cblk"), None),
        check_vma=False,
    )
```

time: 161 us -> 48.5 us (0.30)
  waiting for transfers between devices: 93.4 us -> 0 us
  Pallas kernels: 0 us -> 41.3 us
  matrix products: 23.4 us -> 0 us
  between operations: 13.5 us -> 0.02 us
  other arithmetic: 7.91 us -> 0 us
  starting transfers between devices: 7.28 us -> 0 us
  blocking collectives: 5.78 us -> 0 us
  local copies, waits for them, and re-layouts: 9.65 us -> 6.72 us
    pallas_call x0 -> x2, Pallas kernels: none -> 41.3 us  [the longest x1 39.1 us: per_device(): pl.pallas_call(functools.partial(core_kernel, n, levels, tiles, tile, ran...]
    psum x1 -> x0, waiting for transfers between devices: 36.2 us -> none  [per_device(): summed = lax.psum(leaf_terms(picked, basis), 'cblk')]
    ppermute x4 -> x0, waiting for transfers between devices: 35.6 us -> none  [from_partner(): lax.ppermute(array, axis, [(i, i ^ 1 << bit) for i in range(lax.axis_size...]
    dot_general x12 -> x0, matrix products: 23.4 us -> none  [the longest x2 7.2 us: leaf_terms(): lax.dot_general(data, basis, (((0,), (0,)), ((), ())), preferred_element_...]
    reduce_scatter x1 -> x0, waiting for transfers between devices: 21.5 us -> none  [per_device(): lax.psum_scatter(leaf_terms(weighted, basis), 'cblk', scatter_dimension=0...]
    ppermute x4 -> x0, starting transfers between devices: 7.24 us -> none  [from_partner(): lax.ppermute(array, axis, [(i, i ^ 1 << bit) for i in range(lax.axis_size...]
    unnamed x14, local copies, waits for them, and re-layouts: 0.16 us -> 6.72 us
    select_n x4 -> x0, other arithmetic: 5.92 us -> none  [the longest x2 3.18 us: per_device(): jnp.take(ordered.reshape(tiles, rows // tiles, columns), inverse, axis=0)]
  transfers between devices with their start and end apart: 6 -> 0, of which waited for: 6 -> 0; matrix products, arithmetic and copies ran while one was open for 6% -> 0% of each run, Pallas kernels for 0% -> 0%
where the time goes in v1:
time: 48.5 us; the launch traced here: 48 us
  Pallas kernels  41.3 us (85%)
  local copies, waits for them, and re-layouts  6.72 us (14%)
    pallas_call x1, Pallas kernels, per_device(): pl.pallas_call(functools.partial(core_kernel, n, levels, tiles, tile, ran...  39.1 us
    unnamed x14, local copies, waits for them, and re-layouts  6.72 us
    pallas_call x1, Pallas kernels, per_device(): pl.pallas_call(functools.partial(expand_kernel, tiles, tile, rho), out_sh...  2.18 us

profile of v1, /device:TPU:0, one launch (start us, length us, event | category | flops | bytes accessed | tf_op | source)
XLA Modules:
  0.0 48.0 jit_solution(13590462761751338527)
XLA Ops:
  0.0 0.0 copy-start
  0.0 1.2 %copy-done = bf16[2048,256]{1,0:T(8,128)(2,1)S(1)} copy-done((bf16[2048,256]{1,0:T(8,128)(2,1)S(1)}, bf16[2048,256]{1,0:T(8,128)(2,1)}, u32[]{:S(2)}) %copy-start) | copy-done | bytes 1048600
  1.2 0.0 copy-start.1
  1.2 1.6 %copy-done.1 = bf16[2048,512]{1,0:T(8,128)(2,1)S(1)} copy-done((bf16[2048,512]{1,0:T(8,128)(2,1)S(1)}, bf16[2048,512]{1,0:T(8,128)(2,1)}, u32[]{:S(2)}) %copy-start.1) | copy-done | bytes 2097176
  2.8 0.0 copy-start.2
  2.8 1.0 %copy-done.2 = bf16[2,1,256,512]{3,2,1,0:T(8,128)(2,1)S(1)} copy-done((bf16[2,1,256,512]{3,2,1,0:T(8,128)(2,1)S(1)}, bf16[2,1,256,512]{3,2,1,0:T(8,128)(2,1)}, u32[]{:S(2)}) %copy-start.2) | copy-done | bytes 524312
  3.9 0.0 copy-start.3
  3.9 0.8 %copy-done.3 = f32[16,512]{1,0:T(8,128)S(1)} copy-done((f32[16,512]{1,0:T(8,128)S(1)}, f32[16,512]{1,0:T(8,128)}, u32[]{:S(2)}) %copy-start.3) | copy-done | bytes 32792
  4.6 0.0 copy-start.4
  4.6 0.8 %copy-done.4 = f32[16,512]{1,0:T(8,128)S(1)} copy-done((f32[16,512]{1,0:T(8,128)S(1)}, f32[16,512]{1,0:T(8,128)}, u32[]{:S(2)}) %copy-start.4) | copy-done | bytes 32792
  5.4 0.0 copy-start.5
  5.4 0.7 %copy-done.5 = s32[2048]{0:T(1024)S(1)} copy-done((s32[2048]{0:T(1024)S(1)}, s32[2048]{0:T(1024)}, u32[]{:S(2)}) %copy-start.5) | copy-done | bytes 8216
  6.1 0.0 copy-start.6
  6.1 0.7 %copy-done.6 = s32[1,16]{1,0:T(1,128)S(1)} copy-done((s32[1,16]{1,0:T(1,128)S(1)}, s32[1,16]{1,0:T(1,128)}, u32[]{:S(2)}) %copy-start.6) | copy-done | bytes 88
  6.7 39.1 %butterfly.1.returned = bf16[256,512]{1,0:T(8,128)(2,1)S(1)} custom-call(s32[1,16]{1,0:T(1,128)S(1)} %copy-done.6, s32[16,128]{1,0:T(8,128)S(1)} %bitcast.4, f32[16,512]{1,0:T(8,128)S(1)} %copy-done.3, f32[16,512]{1,0:T(8,128)S(1)} %copy-done.4, bf16[2048,512]{1,0:T(8,128)(2,1)S(1)} %copy-done.1, bf16[16,128,256]{2,1,0:T(8,128)(2,1)S(1)} %bitcast.3, ...), custom_call_target="tpu_custom_call" | custom-call | tf_op jit(solution)/shard_map/butterfly/pallas_call | solution.py:236
  45.8 2.2 %expand.1 = bf16[16,128,512]{2,1,0:T(8,128)(2,1)} custom-call(s32[1,16]{1,0:T(1,128)S(1)} %copy-done.6, bf16[2048,256]{1,0:T(8,128)(2,1)S(1)} %copy-done, bf16[256,512]{1,0:T(8,128)(2,1)S(1)} %butterfly.1.returned), custom_call_target="tpu_custom_call" | custom-call | tf_op jit(solution)/shard_map/expand/pallas_call | solution.py:281
Async XLA Ops:
  0.0 1.2 %copy-start = (bf16[2048,256]{1,0:T(8,128)(2,1)S(1)}, bf16[2048,256]{1,0:T(8,128)(2,1)}, u32[]{:S(2)}) copy-start(bf16[2048,256]{1,0:T(8,128)(2,1)} %basis.1) | copy-start | bytes 3145732
  1.2 1.6 %copy-start.1 = (bf16[2048,512]{1,0:T(8,128)(2,1)S(1)}, bf16[2048,512]{1,0:T(8,128)(2,1)}, u32[]{:S(2)}) copy-start(bf16[2048,512]{1,0:T(8,128)(2,1)} %source_any.1) | copy-start | bytes 6291460
  2.8 1.0 %copy-start.2 = (bf16[2,1,256,512]{3,2,1,0:T(8,128)(2,1)S(1)}, bf16[2,1,256,512]{3,2,1,0:T(8,128)(2,1)}, u32[]{:S(2)}) copy-start(bf16[2,1,256,512]{3,2,1,0:T(8,128)(2,1)} %transfer_any.1) | copy-start | bytes 1572868
  3.9 0.8 %copy-start.3 = (f32[16,512]{1,0:T(8,128)S(1)}, f32[16,512]{1,0:T(8,128)}, u32[]{:S(2)}) copy-start(f32[16,512]{1,0:T(8,128)} %linear.1) | copy-start | bytes 98308
  4.6 0.8 %copy-start.4 = (f32[16,512]{1,0:T(8,128)S(1)}, f32[16,512]{1,0:T(8,128)}, u32[]{:S(2)}) copy-start(f32[16,512]{1,0:T(8,128)} %cubic.1) | copy-start | bytes 98308
  5.4 0.7 %copy-start.5 = (s32[2048]{0:T(1024)S(1)}, s32[2048]{0:T(1024)}, u32[]{:S(2)}) copy-start(s32[2048]{0:T(1024)} %param.11) | copy-start | bytes 24580
  6.1 0.7 %copy-start.6 = (s32[1,16]{1,0:T(1,128)S(1)}, s32[1,16]{1,0:T(1,128)}, u32[]{:S(2)}) copy-start(s32[1,16]{1,0:T(1,128)} %skeleton.3) | copy-start | bytes 196

commit v2 on v1

v2 whole, which is shorter than its diff:
```python
import functools
import math

import jax
import jax.numpy as jnp
from jax import lax
from jax.experimental import pallas as pl
from jax.experimental.pallas import tpu as pltpu
from jax.sharding import PartitionSpec as P

MESH = pl.DeviceIdType.MESH
BF16, F32 = jnp.bfloat16, jnp.float32
PARTS = 2


def mm(left, right):
    return jnp.dot(left, right, preferred_element_type=F32)


def halves(value):
    high = value.astype(BF16)
    return high, (value - high.astype(F32)).astype(BF16)


def inverse_order(skeleton, tiles):
    order = [skeleton[0, i] for i in range(tiles)]
    inverse = []
    for j in range(tiles):
        place = jnp.int32(0)
        for i in range(1, tiles):
            place = jnp.where(order[i] == j, jnp.int32(i), place)
        inverse.append(place)
    return inverse


def core_kernel(
    n, parts, levels, tiles, tile, rank, columns, rho,
    skeleton_any, classes_any, linear_any, cubic_any, source_any, basis_any, transfer_any,
    returned,
    skeleton, classes, linear, cubic,
    source, basis, transfer, flipped, straight, turned, factors_t,
    lin, cub, weighted,
    own32, part_out, part_in, level_out, level_in, share_out, share_in,
    small_sem, local_sem, send_rs, recv_rs, send_lv, recv_lv, send_ag, recv_ag,
):
    wide = columns // parts
    share = wide // n
    rows = tiles * tile
    me = lax.axis_index("cblk")
    seat = lax.axis_index("bfly")

    def peer(k):
        return lax.rem(me + k, n)

    def partner(level):
        step = 1 << level
        return seat + (1 - 2 * lax.rem(seat // step, 2)) * step

    smalls = [
        pltpu.make_async_copy(origin, target, small_sem.at[i])
        for i, (origin, target) in enumerate(
            [(skeleton_any, skeleton), (classes_any, classes), (linear_any, linear), (cubic_any, cubic)]
        )
    ]
    smalls[0].start()
    basis_copy = pltpu.make_async_copy(basis_any, basis, local_sem.at[0])
    basis_copy.start()
    source_copies = [
        pltpu.make_async_copy(
            source_any.at[:, pl.ds(h * wide, wide)], source.at[h], local_sem.at[2 + h]
        )
        for h in range(parts)
    ]
    for copy in source_copies:
        copy.start()
    transfer_copy = pltpu.make_async_copy(transfer_any, transfer, local_sem.at[1])
    transfer_copy.start()
    for copy in smalls[1:]:
        copy.start()

    barrier = pltpu.get_barrier_semaphore()
    for k in range(1, n):
        pl.semaphore_signal(barrier, inc=1, device_id={"cblk": peer(k)}, device_id_type=MESH)
    for level in range(levels):
        pl.semaphore_signal(barrier, inc=1, device_id={"bfly": partner(level)}, device_id_type=MESH)

    smalls[0].wait()
    inverse = inverse_order(skeleton, tiles)
    basis_copy.wait()
    for i in range(tiles):
        flipped[i] = basis[i].T
    for j in range(tiles):
        turned[:, j * tile:(j + 1) * tile] = flipped[inverse[j]]

    def scatter(total, phase, h):
        total = total.T
        copies = []
        for d in range(n):
            piece = total[d * share:(d + 1) * share]
            own32[phase, h, d] = piece
            part_out[phase, h, d] = piece.astype(BF16)
        for k in range(1, n):
            copy = pltpu.make_async_remote_copy(
                src_ref=part_out.at[phase, h, peer(k)],
                dst_ref=part_in.at[phase, h, k - 1],
                send_sem=send_rs.at[phase, h, k - 1],
                recv_sem=recv_rs.at[phase, h, k - 1],
                device_id={"cblk": peer(k)},
                device_id_type=MESH,
            )
            copy.start()
            copies.append(copy)
        return copies

    def collect(copies, phase, h):
        value = own32[phase, h, me]
        for k in range(1, n):
            copies[k - 1].wait_recv()
            value = value + part_in[phase, h, k - 1].astype(F32)
        sent.extend(copies)
        return value

    def exchange(phase, level, h):
        copy = pltpu.make_async_remote_copy(
            src_ref=level_out.at[phase, level, h],
            dst_ref=level_in.at[phase, level, h],
            send_sem=send_lv.at[phase, level, h],
            recv_sem=recv_lv.at[phase, level, h],
            device_id={"bfly": partner(level)},
            device_id_type=MESH,
        )
        copy.start()
        return copy

    def gather(value, phase, h):
        share_out[phase, h] = value.astype(BF16)
        copies = []
        for k in range(1, n):
            copy = pltpu.make_async_remote_copy(
                src_ref=share_out.at[phase, h],
                dst_ref=share_in.at[phase, h, me],
                send_sem=send_ag.at[phase, h, k - 1],
                recv_sem=recv_ag.at[phase, h, k - 1],
                device_id={"cblk": peer(k)},
                device_id_type=MESH,
            )
            copy.start()
            copies.append(copy)
        share_in[phase, h, me] = value.astype(BF16)
        return copies

    def arrive(copies):
        for copy in copies:
            copy.wait_recv()
        sent.extend(copies)

    def doubled(value, factor):
        high, low = halves(value)
        both = mm(jnp.concatenate([high, low], axis=0), factor)
        return both[:share] + both[share:]

    sent = []
    halves_range = range(parts)
    scattered = []
    for h in halves_range:
        source_copies[h].wait()
        total = mm(turned[...], source[h])
        if h == 0:
            pl.semaphore_wait(barrier, n - 1 + levels)
        scattered.append(scatter(total, 0, h))

    transfer_copy.wait()
    for level in range(levels):
        factors_t[level] = transfer[level, 0].T
    for copy in smalls[1:]:
        copy.wait()
    kinds = linear.shape[0]
    pieces = []
    for table in (linear[...], cubic[...]):
        high = table.astype(BF16)
        rest = table - high.astype(F32)
        middle = rest.astype(BF16)
        low = (rest - middle.astype(F32)).astype(BF16)
        pieces.append(jnp.concatenate([high, middle, low], axis=0))
    ids = lax.broadcasted_iota(jnp.int32, (kinds, tile), 0)
    for i in range(tiles):
        hot = jnp.where(classes[i:i + 1, :] == ids, F32(1), F32(0))
        hot = jnp.concatenate([hot, hot, hot], axis=0).T.astype(BF16)
        lin[i * tile:(i + 1) * tile, :] = mm(hot, pieces[0])
        cub[i * tile:(i + 1) * tile, :] = mm(hot, pieces[1])
        straight[:, i * tile:(i + 1) * tile] = flipped[i]

    values = [None] * parts
    for level in range(levels):
        copies = []
        for h in halves_range:
            if level == 0:
                values[h] = collect(scattered[h], 0, h)
            level_out[0, level, h] = values[h].astype(BF16)
            copies.append(exchange(0, level, h))
            values[h] = doubled(values[h], factors_t[level, :rank, :])
        for h in halves_range:
            copies[h].wait_recv()
            values[h] = values[h] + mm(level_in[0, level, h], factors_t[level, rank:, :])
            sent.append(copies[h])
    copies = [gather(values[h], 0, h) for h in halves_range]

    scattered = []
    for h in halves_range:
        arrive(copies[h])
        whole = share_in[0, h].reshape(wide, rank)
        at = slice(h * wide, (h + 1) * wide)
        chunks = 4
        span = rows // chunks
        for c in range(chunks):
            down = slice(c * span, (c + 1) * span)
            left = basis[c * (tiles // chunks):(c + 1) * (tiles // chunks)].reshape(span, rank)
            mapped = rho * lax.dot_general(
                left, whole, (((1,), (1,)), ((), ())), preferred_element_type=F32
            )
            weighted[h, down, :] = (
                mapped * (lin[down, at] + cub[down, at] * mapped * mapped)
            ).astype(BF16)
        scattered.append(scatter(mm(straight[...], weighted[h]), 1, h))

    for level in reversed(range(levels)):
        copies = []
        for h in halves_range:
            if level == levels - 1:
                values[h] = collect(scattered[h], 1, h)
            level_out[1, level, h] = doubled(values[h], transfer[level, 0, :, rank:]).astype(BF16)
            copies.append(exchange(1, level, h))
            values[h] = doubled(values[h], transfer[level, 0, :, :rank])
        for h in halves_range:
            copies[h].wait_recv()
            values[h] = values[h] + level_in[1, level, h].astype(F32)
            sent.append(copies[h])
    copies = [gather(values[h], 1, h) for h in halves_range]
    for h in halves_range:
        arrive(copies[h])
        returned[h] = share_in[1, h]
    for copy in sent:
        copy.wait_send()


def expand_kernel(
    tiles, tile, rho, skeleton_any, basis_any, returned_any, out_any,
    skeleton, basis, returned, ordered, load_sems, sems,
):
    group = 2
    loads = [
        pltpu.make_async_copy(origin, target, load_sems.at[i])
        for i, (origin, target) in enumerate(
            [(returned_any, returned), (basis_any, basis), (skeleton_any, skeleton)]
        )
    ]
    for copy in loads:
        copy.start()
    for copy in loads:
        copy.wait()
    copies = []
    for g in range(tiles // group):
        left = basis[g * group * tile:(g + 1) * group * tile, :]
        value = rho * lax.dot_general(
            left, returned[...], (((1,), (1,)), ((), ())), preferred_element_type=F32
        )
        value = value.astype(BF16)
        for i in range(group):
            at = g * group + i
            ordered[at] = value[i * tile:(i + 1) * tile]
            copy = pltpu.make_async_copy(ordered.at[at], out_any.at[skeleton[0, at]], sems.at[at])
            copy.start()
            copies.append(copy)
    for copy in copies:
        copy.wait()


def per_device(source, basis, transfer, skeleton, row_class, linear_table, cubic_table):
    rows, columns = source.shape
    rank = basis.shape[1]
    tiles = skeleton.shape[1]
    tile = rows // tiles
    levels = transfer.shape[0]
    n = lax.axis_size("cblk")
    parts = PARTS
    wide = columns // parts
    share = wide // n
    rho = math.sqrt(rows * n / rank)
    vmem = pl.BlockSpec(memory_space=pltpu.VMEM)
    anywhere = pl.BlockSpec(memory_space=pl.ANY)
    dma = pltpu.SemaphoreType.DMA
    returned = pl.pallas_call(
        functools.partial(core_kernel, n, parts, levels, tiles, tile, rank, columns, rho),
        out_shape=jax.ShapeDtypeStruct((parts, n, share, rank), BF16),
        in_specs=[anywhere] * 7,
        out_specs=vmem,
        scratch_shapes=[
            pltpu.SMEM(skeleton.shape, jnp.int32),
            pltpu.VMEM((tiles, tile), jnp.int32),
            pltpu.VMEM(linear_table.shape, F32),
            pltpu.VMEM(cubic_table.shape, F32),
            pltpu.VMEM((parts, rows, wide), BF16),
            pltpu.VMEM((tiles, tile, rank), BF16),
            pltpu.VMEM(transfer.shape, BF16),
            pltpu.VMEM((tiles, rank, tile), BF16),
            pltpu.VMEM((rank, rows), BF16),
            pltpu.VMEM((rank, rows), BF16),
            pltpu.VMEM((levels, 2 * rank, rank), BF16),
            pltpu.VMEM((rows, columns), F32),
            pltpu.VMEM((rows, columns), F32),
            pltpu.VMEM((parts, rows, wide), BF16),
            pltpu.VMEM((2, parts, n, share, rank), F32),
            pltpu.VMEM((2, parts, n, share, rank), BF16),
            pltpu.VMEM((2, parts, n - 1, share, rank), BF16),
            pltpu.VMEM((2, levels, parts, share, rank), BF16),
            pltpu.VMEM((2, levels, parts, share, rank), BF16),
            pltpu.VMEM((2, parts, share, rank), BF16),
            pltpu.VMEM((2, parts, n, share, rank), BF16),
            dma((4,)),
            dma((2 + parts,)),
            dma((2, parts, n - 1)),
            dma((2, parts, n - 1)),
            dma((2, levels, parts)),
            dma((2, levels, parts)),
            dma((2, parts, n - 1)),
            dma((2, parts, n - 1)),
        ],
        compiler_params=pltpu.CompilerParams(
            collective_id=0, has_side_effects=True, vmem_limit_bytes=67043328
        ),
        name="butterfly",
    )(
        skeleton,
        row_class.reshape(tiles, tile),
        linear_table,
        cubic_table,
        source,
        basis.reshape(tiles, tile, rank),
        transfer,
    )
    adjoint = pl.pallas_call(
        functools.partial(expand_kernel, tiles, tile, rho),
        out_shape=jax.ShapeDtypeStruct((tiles, tile, columns), BF16),
        in_specs=[anywhere] * 3,
        out_specs=anywhere,
        scratch_shapes=[
            pltpu.SMEM(skeleton.shape, jnp.int32),
            pltpu.VMEM(basis.shape, BF16),
            pltpu.VMEM((columns, rank), BF16),
            pltpu.VMEM((tiles, tile, columns), BF16),
            dma((3,)),
            dma((tiles,)),
        ],
        compiler_params=pltpu.CompilerParams(vmem_limit_bytes=67043328),
        name="expand",
    )(skeleton, basis, returned.reshape(columns, rank))
    return adjoint.reshape(rows, columns)


def solution(mesh):
    placed = (
        P(("ens", "bfly", "cblk"), None),
        P(("ens", "bfly", "cblk"), None),
        P("ens", "bfly", None, None),
        P(("ens", "bfly", "cblk"), None),
        P(("ens", "bfly", "cblk")),
        P(),
        P(),
    )
    return jax.shard_map(
        per_device,
        mesh=mesh,
        in_specs=placed,
        out_specs=P(("ens", "bfly", "cblk"), None),
        check_vma=False,
    )
```

time: 48.5 us -> 39 us (0.80)
  local copies, waits for them, and re-layouts: 6.72 us -> 0 us
  Pallas kernels: 41.3 us -> 38.8 us
    unnamed x14 -> x0, local copies, waits for them, and re-layouts: 6.72 us -> none
    pallas_call x1, Pallas kernels: 39.1 us -> 35.8 us  [per_device(): pl.pallas_call(functools.partial(core_kernel, n, parts, levels, tiles, ti...]
    pallas_call x1, Pallas kernels: 2.18 us -> 3.02 us  [per_device(): pl.pallas_call(functools.partial(expand_kernel, tiles, tile, rho), out_sh...]
where the time goes in v2:
time: 39 us; the launch traced here: 38.8 us
  Pallas kernels  38.8 us (99%)
    pallas_call x1, Pallas kernels, per_device(): pl.pallas_call(functools.partial(core_kernel, n, parts, levels, tiles, ti...  35.8 us
    pallas_call x1, Pallas kernels, per_device(): pl.pallas_call(functools.partial(expand_kernel, tiles, tile, rho), out_sh...  3.02 us

profile of v2, /device:TPU:0, one launch (start us, length us, event | category | flops | bytes accessed | tf_op | source)
XLA Modules:
  0.0 38.8 jit_solution(1348099325429219307)
XLA Ops:
  0.0 35.8 %butterfly.1 = bf16[2,4,64,256]{3,2,1,0:T(8,128)(2,1)} custom-call(s32[1,16]{1,0:T(1,128)} %skeleton_any.3, s32[16,128]{1,0:T(8,128)} %bitcast.6, f32[16,512]{1,0:T(8,128)} %linear_any.1, f32[16,512]{1,0:T(8,128)} %cubic_any.1, bf16[2048,512]{1,0:T(8,128)(2,1)} %source_any.1, bf16[16,128,256]{2,1,0:T(8,128)(2,1)} %bitcast.4, ...), custom_call_target="tpu_custom_call" | custom-call | tf_op jit(solution)/shard_map/butterfly/pallas_call | solution.py:292
  35.8 3.0 %expand.1 = bf16[16,128,512]{2,1,0:T(8,128)(2,1)} custom-call(s32[1,16]{1,0:T(1,128)} %skeleton_any.3, bf16[2048,256]{1,0:T(8,128)(2,1)} %basis_any.1, bf16[512,256]{1,0:T(8,128)(2,1)} %bitcast.5), custom_call_target="tpu_custom_call" | custom-call | tf_op jit(solution)/shard_map/expand/pallas_call | solution.py:341

commit v3 on v2

--- a/solution.py
+++ b/solution.py
@@ -41,7 +41,7 @@
     source, basis, transfer, flipped, straight, turned, factors_t,
     lin, cub, weighted,
     own32, part_out, part_in, level_out, level_in, share_out, share_in,
-    small_sem, local_sem, send_rs, recv_rs, send_lv, recv_lv, send_ag, recv_ag,
+    small_sem, keep_sem, local_sem, send_rs, recv_rs, send_lv, recv_lv, send_ag, recv_ag,
 ):
     wide = columns // parts
     share = wide // n
@@ -55,6 +55,12 @@
     def partner(level):
         step = 1 << level
         return seat + (1 - 2 * lax.rem(seat // step, 2)) * step
+
+    barrier = pltpu.get_barrier_semaphore()
+    for k in range(1, n):
+        pl.semaphore_signal(barrier, inc=1, device_id={"cblk": peer(k)}, device_id_type=MESH)
+    for level in range(levels):
+        pl.semaphore_signal(barrier, inc=1, device_id={"bfly": partner(level)}, device_id_type=MESH)
 
     smalls = [
         pltpu.make_async_copy(origin, target, small_sem.at[i])
@@ -78,12 +84,6 @@
     for copy in smalls[1:]:
         copy.start()
 
-    barrier = pltpu.get_barrier_semaphore()
-    for k in range(1, n):
-        pl.semaphore_signal(barrier, inc=1, device_id={"cblk": peer(k)}, device_id_type=MESH)
-    for level in range(levels):
-        pl.semaphore_signal(barrier, inc=1, device_id={"bfly": partner(level)}, device_id_type=MESH)
-
     smalls[0].wait()
     inverse = inverse_order(skeleton, tiles)
     basis_copy.wait()
@@ -132,13 +132,16 @@
         copy.start()
         return copy
 
+    def landing(phase):
+        return share_in if phase == 0 else returned
+
     def gather(value, phase, h):
         share_out[phase, h] = value.astype(BF16)
         copies = []
         for k in range(1, n):
             copy = pltpu.make_async_remote_copy(
                 src_ref=share_out.at[phase, h],
-                dst_ref=share_in.at[phase, h, me],
+                dst_ref=landing(phase).at[h, me],
                 send_sem=send_ag.at[phase, h, k - 1],
                 recv_sem=recv_ag.at[phase, h, k - 1],
                 device_id={"cblk": peer(k)},
@@ -146,7 +149,12 @@
             )
             copy.start()
             copies.append(copy)
-        share_in[phase, h, me] = value.astype(BF16)
+        if phase == 0:
+            share_in[h, me] = value.astype(BF16)
+        else:
+            keep = pltpu.make_async_copy(share_out.at[1, h], returned.at[h, me], keep_sem.at[h])
+            keep.start()
+            keeps.append(keep)
         return copies
 
     def arrive(copies):
@@ -160,6 +168,7 @@
         return both[:share] + both[share:]
 
     sent = []
+    keeps = []
     halves_range = range(parts)
     scattered = []
     for h in halves_range:
@@ -208,16 +217,14 @@
     scattered = []
     for h in halves_range:
         arrive(copies[h])
-        whole = share_in[0, h].reshape(wide, rank)
+        whole = share_in[h].reshape(wide, rank).T
         at = slice(h * wide, (h + 1) * wide)
         chunks = 4
         span = rows // chunks
         for c in range(chunks):
             down = slice(c * span, (c + 1) * span)
             left = basis[c * (tiles // chunks):(c + 1) * (tiles // chunks)].reshape(span, rank)
-            mapped = rho * lax.dot_general(
-                left, whole, (((1,), (1,)), ((), ())), preferred_element_type=F32
-            )
+            mapped = rho * mm(left, whole)
             weighted[h, down, :] = (
                 mapped * (lin[down, at] + cub[down, at] * mapped * mapped)
             ).astype(BF16)
@@ -238,7 +245,7 @@
     copies = [gather(values[h], 1, h) for h in halves_range]
     for h in halves_range:
         arrive(copies[h])
-        returned[h] = share_in[1, h]
+        keeps[h].wait()
     for copy in sent:
         copy.wait_send()
 
@@ -247,24 +254,27 @@
     tiles, tile, rho, skeleton_any, basis_any, returned_any, out_any,
     skeleton, basis, returned, ordered, load_sems, sems,
 ):
-    group = 2
+    group = 4
+    span = group * tile
     loads = [
         pltpu.make_async_copy(origin, target, load_sems.at[i])
-        for i, (origin, target) in enumerate(
-            [(returned_any, returned), (basis_any, basis), (skeleton_any, skeleton)]
+        for i, (origin, target) in enumerate([(returned_any, returned), (skeleton_any, skeleton)])
+    ]
+    loads += [
+        pltpu.make_async_copy(
+            basis_any.at[pl.ds(g * span, span)], basis.at[pl.ds(g * span, span)], load_sems.at[2 + g]
         )
+        for g in range(tiles // group)
     ]
     for copy in loads:
         copy.start()
-    for copy in loads:
-        copy.wait()
+    loads[0].wait()
+    right = returned[...].T
+    loads[1].wait()
     copies = []
     for g in range(tiles // group):
-        left = basis[g * group * tile:(g + 1) * group * tile, :]
-        value = rho * lax.dot_general(
-            left, returned[...], (((1,), (1,)), ((), ())), preferred_element_type=F32
-        )
-        value = value.astype(BF16)
+        loads[2 + g].wait()
+        value = (rho * mm(basis[g * span:(g + 1) * span, :], right)).astype(BF16)
         for i in range(group):
             at = g * group + i
             ordered[at] = value[i * tile:(i + 1) * tile]
@@ -286,14 +296,13 @@
     wide = columns // parts
     share = wide // n
     rho = math.sqrt(rows * n / rank)
-    vmem = pl.BlockSpec(memory_space=pltpu.VMEM)
     anywhere = pl.BlockSpec(memory_space=pl.ANY)
     dma = pltpu.SemaphoreType.DMA
     returned = pl.pallas_call(
         functools.partial(core_kernel, n, parts, levels, tiles, tile, rank, columns, rho),
         out_shape=jax.ShapeDtypeStruct((parts, n, share, rank), BF16),
         in_specs=[anywhere] * 7,
-        out_specs=vmem,
+        out_specs=anywhere,
         scratch_shapes=[
             pltpu.SMEM(skeleton.shape, jnp.int32),
             pltpu.VMEM((tiles, tile), jnp.int32),
@@ -315,8 +324,9 @@
             pltpu.VMEM((2, levels, parts, share, rank), BF16),
             pltpu.VMEM((2, levels, parts, share, rank), BF16),
             pltpu.VMEM((2, parts, share, rank), BF16),
-            pltpu.VMEM((2, parts, n, share, rank), BF16),
+            pltpu.VMEM((parts, n, share, rank), BF16),
             dma((4,)),
+            dma((parts,)),
             dma((2 + parts,)),
             dma((2, parts, n - 1)),
             dma((2, parts, n - 1)),
@@ -348,7 +358,7 @@
             pltpu.VMEM(basis.shape, BF16),
             pltpu.VMEM((columns, rank), BF16),
             pltpu.VMEM((tiles, tile, columns), BF16),
-            dma((3,)),
+            dma((2 + tiles // 4,)),
             dma((tiles,)),
         ],
         compiler_params=pltpu.CompilerParams(vmem_limit_bytes=67043328),

time: 39 us -> 38.6 us (0.990)
    pallas_call x1, Pallas kernels: 35.8 us -> 35.2 us  [per_device(): pl.pallas_call(functools.partial(core_kernel, n, parts, levels, tiles, ti...]
where the time goes in v3:
time: 38.6 us; the launch traced here: 38.5 us
  Pallas kernels  38.5 us (100%)
    pallas_call x1, Pallas kernels, per_device(): pl.pallas_call(functools.partial(core_kernel, n, parts, levels, tiles, ti...  35.2 us
    pallas_call x1, Pallas kernels, per_device(): pl.pallas_call(functools.partial(expand_kernel, tiles, tile, rho), out_sh...  3.24 us

profile of v3, /device:TPU:0, one launch (start us, length us, event | category | flops | bytes accessed | tf_op | source)
XLA Modules:
  0.0 38.5 jit_solution(10647817990231102526)
XLA Ops:
  0.0 35.2 %butterfly.1 = bf16[2,4,64,256]{3,2,1,0:T(8,128)(2,1)} custom-call(s32[1,16]{1,0:T(1,128)} %skeleton_any.3, s32[16,128]{1,0:T(8,128)} %bitcast.6, f32[16,512]{1,0:T(8,128)} %linear_any.1, f32[16,512]{1,0:T(8,128)} %cubic_any.1, bf16[2048,512]{1,0:T(8,128)(2,1)} %source_any.1, bf16[16,128,256]{2,1,0:T(8,128)(2,1)} %bitcast.4, ...), custom_call_target="tpu_custom_call" | custom-call | tf_op jit(solution)/shard_map/butterfly/pallas_call | solution.py:301
  35.2 3.2 %expand.1 = bf16[16,128,512]{2,1,0:T(8,128)(2,1)} custom-call(s32[1,16]{1,0:T(1,128)} %skeleton_any.3, bf16[2048,256]{1,0:T(8,128)(2,1)} %basis_any.1, bf16[512,256]{1,0:T(8,128)(2,1)} %bitcast.5), custom_call_target="tpu_custom_call" | custom-call | tf_op jit(solution)/shard_map/expand/pallas_call | solution.py:351

commit v4 on v3

--- a/solution.py
+++ b/solution.py
@@ -260,21 +260,16 @@
         pltpu.make_async_copy(origin, target, load_sems.at[i])
         for i, (origin, target) in enumerate([(returned_any, returned), (skeleton_any, skeleton)])
     ]
-    loads += [
-        pltpu.make_async_copy(
-            basis_any.at[pl.ds(g * span, span)], basis.at[pl.ds(g * span, span)], load_sems.at[2 + g]
-        )
-        for g in range(tiles // group)
-    ]
+    loads.append(pltpu.make_async_copy(basis_any, basis, load_sems.at[2]))
     for copy in loads:
         copy.start()
     loads[0].wait()
-    right = returned[...].T
     loads[1].wait()
     copies = []
     for g in range(tiles // group):
-        loads[2 + g].wait()
-        value = (rho * mm(basis[g * span:(g + 1) * span, :], right)).astype(BF16)
+        if g == 0:
+            loads[2].wait()
+        value = (rho * lax.dot_general(basis[g * span:(g + 1) * span, :], returned[...], (((1,), (1,)), ((), ())), preferred_element_type=F32)).astype(BF16)
         for i in range(group):
             at = g * group + i
             ordered[at] = value[i * tile:(i + 1) * tile]
@@ -358,7 +353,7 @@
             pltpu.VMEM(basis.shape, BF16),
             pltpu.VMEM((columns, rank), BF16),
             pltpu.VMEM((tiles, tile, columns), BF16),
-            dma((2 + tiles // 4,)),
+            dma((3,)),
             dma((tiles,)),
         ],
         compiler_params=pltpu.CompilerParams(vmem_limit_bytes=67043328),

time: 38.6 us -> 38.4 us (level)
  no operation moved by 1% of the time
where the time goes in v4:
time: 38.4 us; the launch traced here: 38.2 us
  Pallas kernels  38.2 us (99%)
    pallas_call x1, Pallas kernels, per_device(): pl.pallas_call(functools.partial(core_kernel, n, parts, levels, tiles, ti...  35.2 us
    pallas_call x1, Pallas kernels, per_device(): pl.pallas_call(functools.partial(expand_kernel, tiles, tile, rho), out_sh...  3.01 us

profile of v4, /device:TPU:0, one launch (start us, length us, event | category | flops | bytes accessed | tf_op | source)
XLA Modules:
  0.0 38.2 jit_solution(18292068732748800489)
XLA Ops:
  0.0 35.2 %butterfly.1 = bf16[2,4,64,256]{3,2,1,0:T(8,128)(2,1)} custom-call(s32[1,16]{1,0:T(1,128)} %skeleton_any.3, s32[16,128]{1,0:T(8,128)} %bitcast.6, f32[16,512]{1,0:T(8,128)} %linear_any.1, f32[16,512]{1,0:T(8,128)} %cubic_any.1, bf16[2048,512]{1,0:T(8,128)(2,1)} %source_any.1, bf16[16,128,256]{2,1,0:T(8,128)(2,1)} %bitcast.4, ...), custom_call_target="tpu_custom_call" | custom-call | tf_op jit(solution)/shard_map/butterfly/pallas_call | solution.py:296
  35.2 3.0 %expand.1 = bf16[16,128,512]{2,1,0:T(8,128)(2,1)} custom-call(s32[1,16]{1,0:T(1,128)} %skeleton_any.3, bf16[2048,256]{1,0:T(8,128)(2,1)} %basis_any.1, bf16[512,256]{1,0:T(8,128)(2,1)} %bitcast.5), custom_call_target="tpu_custom_call" | custom-call | tf_op jit(solution)/shard_map/expand/pallas_call | solution.py:346
